TPU v7x, 32 devices: a whole 2x2x4 slice. The times are simulated.
32 devices in a mesh: dp: 8 (over z, y), tensor: 4 (over x, core).
Axes of the slice: x: 2, y: 2, z: 4, core: 2. Of those that a mesh axis runs over, the one named last changes fastest.
Arguments:
- query: bfloat16 [64, 64, 128], P('dp', 'tensor'), may hold values from -8 to 8
- kv_pages: bfloat16 [560, 8, 2, 128, 128], P('dp', 'tensor'), may hold values from -8 to 8
- move_plan: int32 [8, 3, 12], P('dp'), may hold values from 0 to 69, as said below
- move_count: int32 [8], P('dp'), may hold values from 9 to 12
- block_table: int32 [64, 8], P('dp'), may hold values from 0 to 69, as said below
- seq_lens: int32 [64], P('dp'), may hold values from 1 to 1024
- out_weight: bfloat16 [8192, 8192], P('tensor', 'dp'), may hold values from -0.0625 to 0.0625
Outputs:
- new_pages: bfloat16 [560, 8, 2, 128, 128], P('dp', 'tensor')
- projected: bfloat16 [64, 8192], P(None, 'dp')
Inputs may be any that keep to these rules, and one draw needn't show every extreme that they name: `move_plan`: row 0 holds the device's own source slots, distinct within a device; row 1 target devices; row 2 target slots. Entries at or past the device's move_count are padding to be ignored. At most 2 valid moves go from one device to one device, and some pair has exactly 2. The (target device, target slot) pairs of all valid moves are distinct. `block_table`: all entries of the sequences of one device are distinct slots of that device; sequence s belongs to device s // 8.
All inputs are finite; a program needn't handle non-finite values.
Results may differ from a plain program's by a relative error of at most 0.0055.
Values may be sent and summed in bfloat16 or wider, within the bound.
No kernel may reach another device: no remote copies, remote signals or barrier semaphores. Data moves between devices by JAX's collectives and lax.ppermute only.
A program may use at most 128 MiB of HBM per device.

v0:
```python
import math
import jax
import jax.numpy as jnp
from jax import lax
from jax.sharding import PartitionSpec as P

HD = 128
BLOCK = 128
BLOCKS = 8
CAP = 2


def body(query, kv_pages, move_plan, move_count, block_table, seq_lens, out_weight):
    slots_here = kv_pages.shape[0]
    move_total = move_plan.shape[2]
    devices = lax.axis_size("dp")
    capacity = CAP
    holding_rows = devices * capacity
    move_list = move_plan[0]
    move_index = jnp.arange(move_total, dtype=jnp.int32)
    is_valid = move_index < move_count[0]
    target_dev = move_list[1]
    earlier = (
        (target_dev[:, None] == target_dev[None, :])
        & is_valid[None, :]
        & (move_index[None, :] < move_index[:, None])
    )
    dest_rank = jnp.sum(earlier.astype(jnp.int32), axis=1)
    send_row = jnp.where(is_valid, target_dev * capacity + dest_rank, -1)
    flat_pages = kv_pages.reshape(slots_here, -1)
    picked = flat_pages[move_list[0]]
    select = jnp.arange(holding_rows, dtype=jnp.int32)[:, None] == send_row[None, :]
    outgoing = jnp.dot(
        select.astype(jnp.bfloat16), picked, preferred_element_type=jnp.float32
    ).astype(jnp.bfloat16)
    outgoing = outgoing.reshape((holding_rows,) + kv_pages.shape[1:])
    out_slots = jnp.sum(select.astype(jnp.int32) * (move_list[2][None, :] + 1), axis=1) - 1
    slot_tags = out_slots.astype(jnp.float32).astype(jnp.bfloat16)
    arrived, arrived_tags = (
        lax.all_to_all(outgoing, "dp", split_axis=0, concat_axis=0, tiled=True),
        lax.all_to_all(slot_tags, "dp", split_axis=0, concat_axis=0, tiled=True),
    )
    incoming = arrived_tags.astype(jnp.float32).astype(jnp.int32)
    hit_table = jnp.arange(slots_here, dtype=jnp.int32)[:, None] == incoming[None, :]
    placed = jnp.dot(
        hit_table.astype(jnp.bfloat16),
        arrived.reshape(holding_rows, -1),
        preferred_element_type=jnp.float32,
    ).astype(jnp.bfloat16)
    written = jnp.any(hit_table, axis=1)
    new_pages = jnp.where(written[:, None], placed, flat_pages).reshape(kv_pages.shape)
    seq_here = query.shape[0]
    local_heads = new_pages.shape[1]
    head_dim = query.shape[2]
    group_size = query.shape[1] // local_heads
    context = BLOCKS * BLOCK
    gathered = new_pages[block_table]
    key_rows = jnp.transpose(gathered[:, :, :, 0], (0, 2, 1, 3, 4)).reshape(
        seq_here, local_heads, context, head_dim
    )
    value_rows = jnp.transpose(gathered[:, :, :, 1], (0, 2, 1, 3, 4)).reshape(
        seq_here, local_heads, context, head_dim
    )
    grouped = query.reshape(seq_here, local_heads, group_size, head_dim)
    score_scale = 1.0 / math.sqrt(HD)
    scores = (
        jnp.einsum("skgd,sktd->skgt", grouped, key_rows, preferred_element_type=jnp.float32)
        * score_scale
    )
    position = jnp.arange(context, dtype=jnp.int32)
    scores = jnp.where(position[None, None, None, :] < seq_lens[:, None, None, None], scores, -1e30)
    largest = jnp.max(scores, axis=-1, keepdims=True)
    expo = jnp.exp(scores - largest)
    weights = (expo / jnp.sum(expo, axis=-1, keepdims=True)).astype(jnp.bfloat16)
    mixed_heads = jnp.einsum(
        "skgt,sktd->skgd", weights, value_rows, preferred_element_type=jnp.float32
    )
    attention = mixed_heads.reshape(seq_here, local_heads * group_size * head_dim).astype(
        jnp.bfloat16
    )
    partial_sums = jnp.dot(
        lax.all_gather(attention, "dp", axis=0, tiled=True),
        out_weight,
        preferred_element_type=jnp.float32,
    )
    summed = lax.psum(partial_sums, "tensor")
    return (new_pages, summed.astype(jnp.bfloat16))


def solution(mesh):
    placed = (
        P("dp", "tensor", None),
        P("dp", "tensor", None, None, None),
        P("dp", None, None),
        P("dp"),
        P("dp", None),
        P("dp"),
        P("tensor", "dp"),
    )
    return jax.shard_map(
        body,
        mesh=mesh,
        in_specs=placed,
        out_specs=(P("dp", "tensor", None, None, None), P(None, "dp")),
        check_vma=False,
    )
```

profile of v0, /device:TPU:1, one launch (start us, length us, event | category | flops | bytes accessed | tf_op | source)
XLA Modules:
  0.0 194.9 jit_solution(8297206147046076033)
XLA Ops:
  0.6 0.0 copy-start
  0.6 0.7 slice_bitcast_fusion
  2.0 0.2 convert_reduce_fusion
  2.2 0.7 add_select_fusion
  2.8 0.1 select_reduce_fusion
  3.0 0.7 convert_element_type.79
  3.7 6.4 %all-to-all-start = ((bf16[8,2,1]{1,2,0:T(2,128)(2,1)}), bf16[8,2,1]{1,2,0:T(2,128)(2,1)S(1)}, u32[]{:S(2)}, u32[]{:S(2)}) async-start(bf16[8,2,1]{1,2,0:T(2,128)(2,1)} %convert_element_type.79), calls=%async_computation | async-start | bytes 8192 | tf_op jit(solution)/shard_map/all_to_all | solution.py:41
  10.0 0.7 fusion.16
  10.7 8.8 %pad.2 = bf16[72,512,128]{2,1,0:T(8,128)(2,1)} pad(bf16[70,512,128]{2,1,0:T(8,128)(2,1)} %bitcast.69, bf16[]{:T(256)} %constant.38), padding=0_2x0_0x0_0 | pad | bytes 18612226
  19.5 13.8 %copy.21 = bf16[9,8,512,128]{3,1,2,0:T(8,128)(2,1)} copy(bf16[9,8,512,128]{3,2,1,0:T(8,128)(2,1)} %bitcast.62) | data formatting | bytes 18874368
  33.3 7.8 %gather_fusion = bf16[12,65536]{1,0:T(8,128)(2,1)S(1)} fusion(bf16[70,65536]{1,0:T(8,128)(2,1)} %bitcast.59, s32[1024]{0:T(1024)S(1)} %pad_clamp_fusion.1), kind=kCustom, calls=%fused_computation | custom fusion | bytes 3145776 | tf_op jit(solution)/shard_map/gather | solution.py:31
  41.1 0.7 fusion.4
  41.8 0.0 copy-start.1
  41.8 0.0 copy-start.2
  41.8 1.9 copy.22
  43.7 0.0 all-to-all-done
  43.7 5.4 %all-to-all-start.1 = ((bf16[16,2,2,128,128]{4,3,2,1,0:T(8,128)(2,1)}), bf16[16,2,2,128,128]{4,3,2,1,0:T(8,128)(2,1)S(1)}, u32[]{:S(2)}, u32[]{:S(2)}) async-start(bf16[16,2,2,128,128]{4,3,2,1,0:T(8,128)(2,1)} %bitcast.24), calls=%async_computation.1 | async-start | bytes 4194304 | tf_op jit(solution)/shard_map/all_to_all | solution.py:40
  49.2 0.0 copy-done.1
  49.2 0.1 reshape.158
  49.3 0.0 copy-done.2
  49.3 0.1 iota_compare_fusion
  49.4 0.1 convert_element_type.72
  49.4 0.1 fusion.12
  49.5 46.5 %all-to-all-done.1 = bf16[16,2,2,128,128]{4,3,2,1,0:T(8,128)(2,1)S(1)} async-done(((bf16[16,2,2,128,128]{4,3,2,1,0:T(8,128)(2,1)}), bf16[16,2,2,128,128]{4,3,2,1,0:T(8,128)(2,1)S(1)}, u32[]{:S(2)}, u32[]{:S(2)}) %all-to-all-start.1) | async-done | bytes 2097184 | tf_op jit(solution)/shard_map/all_to_all | solution.py:40
  96.0 10.8 %fusion.1 = bf16[70,65536]{1,0:T(8,128)(2,1)} fusion(bf16[70,65536]{1,0:T(8,128)(2,1)} %bitcast.60, pred[70]{0:T(512)(128)(4,1)S(1)} %fusion.12, bf16[2,8,512,128]{3,2,1,0:T(8,128)(2,1)S(1)} %bitcast.70, s32[16]{0:T(128)S(1)} %convert_element_type.72), kind=kOutput, calls=%fused_computation.4 | convolution fusion | flops 155976800 | bytes 20447366 | tf_op jit(solution)/shard_map/dot_general | solution.py:45
  106.8 9.9 %copy.24 = bf16[9,8,512,128]{3,2,1,0:T(8,128)(2,1)} copy(bf16[9,8,512,128]{3,1,2,0:T(8,128)(2,1)} %bitcast.61) | data formatting | bytes 18874368
  116.7 8.4 %slice.29 = bf16[70,512,128]{2,1,0:T(8,128)(2,1)} slice(bf16[72,512,128]{2,1,0:T(8,128)(2,1)} %bitcast.63), slice={[0:70], [0:512], [0:128]} | slice | bytes 18350080
  125.1 9.1 %gather_fusion.1 = bf16[64,2,2,128,128]{4,3,2,1,0:T(8,128)(2,1)} fusion(bf16[70,2,2,128,128]{4,3,2,1,0:T(8,128)(2,1)} %bitcast.64, s32[1024]{0:T(1024)S(1)} %pad_clamp_fusion), kind=kCustom, calls=%fused_computation.1 | custom fusion | bytes 16777472 | tf_op jit(solution)/shard_map/gather | solution.py:57
  134.2 3.8 %fusion.17 = (bf16[8,8,2,1,128,128]{5,4,3,2,1,0:T(8,128)(2,1)S(1)}, bf16[8,8,2,1,128,128]{5,4,3,2,1,0:T(8,128)(2,1)S(1)}) fusion(bf16[8,8,2,2,128,128]{5,4,3,2,1,0:T(8,128)(2,1)} %bitcast.66), kind=kLoop, calls=%fused_computation.41 | loop fusion | bytes 16777216 | tf_op jit(solution)/shard_map/slice | solution.py:58
  138.1 0.6 copy.19
  138.6 0.0 copy-done
  138.7 1.2 fusion.8
  139.8 0.3 fusion.18
  140.1 2.2 %copy.20 = bf16[8,8,2,1,128,128]{5,4,1,2,0,3:T(8,128)(2,1)} copy(bf16[8,8,2,1,128,128]{5,4,3,2,1,0:T(8,128)(2,1)S(1)} %get-tuple-element.3) | data formatting | bytes 8388608
  142.3 2.9 %fusion.9 = bf16[1,8,16,128]{3,2,1,0:T(8,128)(2,1)S(1)} fusion(bf16[8,2,1024,128]{3,2,1,0:T(8,128)(2,1)} %bitcast.67, f32[8,2,8]{2,1,0:T(2,128)S(1)} %fusion.18, f32[8,2,8,1024]{3,2,1,0:T(8,128)S(1)} %fusion.8), kind=kOutput, calls=%fused_computation.15 | convolution fusion | flops 33965184 | bytes 4751872 | tf_op jit(solution)/shard_map/skgt,sktd->skgd/dot_general | solution.py:75
  145.3 25.4 %all_gather.3 = bf16[64,2048]{1,0:T(8,128)(2,1)S(1)} all-gather(bf16[8,2048]{1,0:T(8,128)(2,1)S(1)} %bitcast.71), channel_id=1, replica_groups=mesh['dp'=8,'tensor'=4] {'dp'}, dimensions={0}, use_global_device_ids=true | all-gather | bytes 294912 | tf_op jit(solution)/shard_map/all_gather | solution.py:82
  170.7 3.0 %fusion.19 = f32[64,1024]{1,0:T(8,128)S(1)} fusion(bf16[64,2048]{1,0:T(8,128)(2,1)S(1)} %all_gather.3, bf16[2048,1024]{1,0:T(8,128)(2,1)} %param.13), kind=kOutput, calls=%fused_computation.43 | convolution fusion | flops 268435456 | bytes 4718592 | tf_op jit(solution)/shard_map/dot_general | solution.py:81
  173.7 21.2 %all-reduce.1 = bf16[64,1024]{1,0:T(8,128)(2,1)} all-reduce(f32[64,1024]{1,0:T(8,128)S(1)} %fusion.19), channel_id=1, replica_groups=mesh['dp'=8,'tensor'=4] {'tensor'}, use_global_device_ids=true, to_apply=%region_5.6 | all-reduce | flops 65536 | bytes 393216 | tf_op jit(solution)/shard_map/psum | solution.py:86
  (7 shorter events, 0.1 us)
Async XLA Ops:
  0.6 138.0 %copy-start = (bf16[8,16,128]{2,1,0:T(8,128)(2,1)S(1)}, bf16[8,16,128]{2,1,0:T(8,128)(2,1)}, u32[]{:S(2)}) copy-start(bf16[8,16,128]{2,1,0:T(8,128)(2,1)} %param.7) | copy-start | bytes 98308
  3.7 40.1 %all-to-all-start = ((bf16[8,2,1]{1,2,0:T(2,128)(2,1)}), bf16[8,2,1]{1,2,0:T(2,128)(2,1)S(1)}, u32[]{:S(2)}, u32[]{:S(2)}) async-start(bf16[8,2,1]{1,2,0:T(2,128)(2,1)} %convert_element_type.79), calls=%async_computation | async-start | bytes 8192 | tf_op jit(solution)/shard_map/all_to_all | solution.py:41
  41.8 7.3 %copy-start.1 = (s32[8,8]{1,0:T(8,128)S(1)}, s32[8,8]{1,0:T(8,128)}, u32[]{:S(2)}) copy-start(s32[8,8]{1,0:T(8,128)} %param.11) | copy-start | bytes 772
  41.8 7.4 %copy-start.2 = (s32[8]{0:T(128)S(1)}, s32[8]{0:T(128)}, u32[]{:S(2)}) copy-start(s32[8]{0:T(128)} %param.12) | copy-start | bytes 100
  43.7 52.3 %all-to-all-start.1 = ((bf16[16,2,2,128,128]{4,3,2,1,0:T(8,128)(2,1)}), bf16[16,2,2,128,128]{4,3,2,1,0:T(8,128)(2,1)S(1)}, u32[]{:S(2)}, u32[]{:S(2)}) async-start(bf16[16,2,2,128,128]{4,3,2,1,0:T(8,128)(2,1)} %bitcast.24), calls=%async_computation.1 | async-start | bytes 4194304 | tf_op jit(solution)/shard_map/all_to_all | solution.py:40
where the time goes:
time: 196 us; the launch traced here: 195 us
  local copies, waits for them, and re-layouts  67.2 us (34%)
  blocking collectives  46.6 us (24%)
  waiting for transfers between devices  46.5 us (24%)
  matrix products  18.6 us (9%)
  starting transfers between devices  11.8 us (6%)
  other arithmetic  2.78 us (1%)
    all_to_all x1, waiting for transfers between devices, body(): lax.all_to_all(outgoing, 'dp', split_axis=0, concat_axis=0, tiled=True)  46.5 us
    unnamed x14, local copies, waits for them, and re-layouts  45.6 us
    all_gather x1, blocking collectives, body(): lax.all_gather(attention, 'dp', axis=0, tiled=True)  25.4 us
    psum x1, blocking collectives, body(): summed = lax.psum(partial_sums, 'tensor')  21.2 us
    dot_general x1, matrix products, body(): jnp.dot(hit_table.astype(jnp.bfloat16), arrived.reshape(holding_rows, -1)...  10.8 us
    gather x1, local copies, waits for them, and re-layouts, body(): gathered = new_pages[block_table]  9.14 us
    gather x1, local copies, waits for them, and re-layouts, body(): picked = flat_pages[move_list[0]]  7.81 us
    all_to_all x1, starting transfers between devices, body(): lax.all_to_all(slot_tags, 'dp', split_axis=0, concat_axis=0, tiled=True)  6.37 us
  transfers between devices with their start and end apart: 2, of which 1 were waited for; matrix products, arithmetic and copies ran while one was open for 17% of the time, Pallas kernels for 0%

commit v1 on v0

--- a/solution.py
+++ b/solution.py
@@ -8,6 +8,16 @@
 BLOCK = 128
 BLOCKS = 8
 CAP = 2
+
+
+def ring_gather(x, axis, dim):
+    ways, here, lap = (lax.axis_size(axis), lax.axis_index(axis), x.shape[dim])
+    shape = [n * ways if d == dim else n for d, n in enumerate(x.shape)]
+    full = lax.dynamic_update_slice_in_dim(jnp.zeros(shape, x.dtype), x, here * lap, axis=dim)
+    for far in range(1, ways):
+        x = lax.ppermute(x, axis, [(d, (d + 1) % ways) for d in range(ways)])
+        full = lax.dynamic_update_slice_in_dim(full, x, (here - far) % ways * lap, axis=dim)
+    return full
 
 
 def body(query, kv_pages, move_plan, move_count, block_table, seq_lens, out_weight):
@@ -79,9 +89,7 @@
         jnp.bfloat16
     )
     partial_sums = jnp.dot(
-        lax.all_gather(attention, "dp", axis=0, tiled=True),
-        out_weight,
-        preferred_element_type=jnp.float32,
+        ring_gather(attention, "dp", 0), out_weight, preferred_element_type=jnp.float32
     )
     summed = lax.psum(partial_sums, "tensor")
     return (new_pages, summed.astype(jnp.bfloat16))

time: 196 us -> 211 us (1.077)
  waiting for transfers between devices: 46.5 us -> 82.5 us
  blocking collectives: 46.6 us -> 23.9 us
  starting transfers between devices: 11.8 us -> 14 us
    ppermute x0 -> x7, waiting for transfers between devices: none -> 36 us  [ring_gather(): x = lax.ppermute(x, axis, [(d, (d + 1) % ways) for d in range(ways)])]
    all_gather x1 -> x0, blocking collectives: 25.4 us -> none  [body(): lax.all_gather(attention, 'dp', axis=0, tiled=True)]
    psum x1, blocking collectives: 21.2 us -> 23.9 us  [body(): summed = lax.psum(partial_sums, 'tensor')]
    ppermute x0 -> x7, starting transfers between devices: none -> 2.17 us  [ring_gather(): x = lax.ppermute(x, axis, [(d, (d + 1) % ways) for d in range(ways)])]
  transfers between devices with their start and end apart: 2 -> 9, of which waited for: 1 -> 8; matrix products, arithmetic and copies ran while one was open for 17% -> 16% of each run, Pallas kernels for 0% -> 0%
where the time goes in v1:
time: 211 us
  waiting for transfers between devices  82.5 us (39%)
  local copies, waits for them, and re-layouts  67.3 us (32%)
  blocking collectives  23.9 us (11%)
  matrix products  18.6 us (9%)
  starting transfers between devices  14 us (7%)
  other arithmetic  2.78 us (1%)
    all_to_all x1, waiting for transfers between devices, body(): lax.all_to_all(outgoing, 'dp', split_axis=0, concat_axis=0, tiled=True)  46.5 us
    unnamed x14, local copies, waits for them, and re-layouts  45.6 us
    ppermute x7, waiting for transfers between devices, ring_gather(): x = lax.ppermute(x, axis, [(d, (d + 1) % ways) for d in range(ways)])  36 us
    psum x1, blocking collectives, body(): summed = lax.psum(partial_sums, 'tensor')  23.9 us
    dot_general x1, matrix products, body(): jnp.dot(hit_table.astype(jnp.bfloat16), arrived.reshape(holding_rows, -1)...  10.8 us
    gather x1, local copies, waits for them, and re-layouts, body(): gathered = new_pages[block_table]  9.14 us
    gather x1, local copies, waits for them, and re-layouts, body(): picked = flat_pages[move_list[0]]  7.81 us
    all_to_all x1, starting transfers between devices, body(): lax.all_to_all(slot_tags, 'dp', split_axis=0, concat_axis=0, tiled=True)  6.37 us
  transfers between devices with their start and end apart: 9, of which 8 were waited for; matrix products, arithmetic and copies ran while one was open for 16% of the time, Pallas kernels for 0%

profile of v1, /device:TPU:1, one launch (start us, length us, event | category | flops | bytes accessed | tf_op | source)
XLA Modules:
  0.0 210.5 jit_solution(10932892603627373487)
XLA Ops:
  0.6 0.0 copy-start
  0.6 0.7 slice_bitcast_fusion
  2.0 0.2 convert_reduce_fusion
  2.2 0.7 add_select_fusion
  2.8 0.1 select_reduce_fusion
  3.0 0.7 convert_element_type.79
  3.7 6.4 %all-to-all-start = ((bf16[8,2,1]{1,2,0:T(2,128)(2,1)}), bf16[8,2,1]{1,2,0:T(2,128)(2,1)S(1)}, u32[]{:S(2)}, u32[]{:S(2)}) async-start(bf16[8,2,1]{1,2,0:T(2,128)(2,1)} %convert_element_type.79), calls=%async_computation | async-start | bytes 8192 | tf_op jit(solution)/shard_map/all_to_all | solution.py:51
  10.0 0.7 fusion.16
  10.7 8.8 %pad.2 = bf16[72,512,128]{2,1,0:T(8,128)(2,1)} pad(bf16[70,512,128]{2,1,0:T(8,128)(2,1)} %bitcast.71, bf16[]{:T(256)} %constant.76.clone.1), padding=0_2x0_0x0_0 | pad | bytes 18612226
  19.5 13.8 %copy.21 = bf16[9,8,512,128]{3,1,2,0:T(8,128)(2,1)} copy(bf16[9,8,512,128]{3,2,1,0:T(8,128)(2,1)} %bitcast.64) | data formatting | bytes 18874368
  33.3 7.8 %gather_fusion = bf16[12,65536]{1,0:T(8,128)(2,1)S(1)} fusion(bf16[70,65536]{1,0:T(8,128)(2,1)} %bitcast.61, s32[1024]{0:T(1024)S(1)} %pad_clamp_fusion.1), kind=kCustom, calls=%fused_computation | custom fusion | bytes 3145776 | tf_op jit(solution)/shard_map/gather | solution.py:41
  41.1 0.7 fusion.4
  41.8 0.0 copy-start.1
  41.8 0.0 copy-start.2
  41.8 1.9 copy.22
  43.7 0.0 all-to-all-done
  43.7 5.4 %all-to-all-start.1 = ((bf16[16,2,2,128,128]{4,3,2,1,0:T(8,128)(2,1)}), bf16[16,2,2,128,128]{4,3,2,1,0:T(8,128)(2,1)S(1)}, u32[]{:S(2)}, u32[]{:S(2)}) async-start(bf16[16,2,2,128,128]{4,3,2,1,0:T(8,128)(2,1)} %bitcast.24), calls=%async_computation.1 | async-start | bytes 4194304 | tf_op jit(solution)/shard_map/all_to_all | solution.py:50
  49.2 0.1 reshape.158
  49.3 0.1 iota_compare_fusion
  49.4 0.1 convert_element_type.72
  49.4 0.1 fusion.12
  49.5 46.5 %all-to-all-done.1 = bf16[16,2,2,128,128]{4,3,2,1,0:T(8,128)(2,1)S(1)} async-done(((bf16[16,2,2,128,128]{4,3,2,1,0:T(8,128)(2,1)}), bf16[16,2,2,128,128]{4,3,2,1,0:T(8,128)(2,1)S(1)}, u32[]{:S(2)}, u32[]{:S(2)}) %all-to-all-start.1) | async-done | bytes 2097184 | tf_op jit(solution)/shard_map/all_to_all | solution.py:50
  96.0 10.8 %fusion.1 = bf16[70,65536]{1,0:T(8,128)(2,1)} fusion(bf16[70,65536]{1,0:T(8,128)(2,1)} %bitcast.62, pred[70]{0:T(512)(128)(4,1)S(1)} %fusion.12, bf16[2,8,512,128]{3,2,1,0:T(8,128)(2,1)S(1)} %bitcast.72, s32[16]{0:T(128)S(1)} %convert_element_type.72), kind=kOutput, calls=%fused_computation.4 | convolution fusion | flops 155976800 | bytes 20447366 | tf_op jit(solution)/shard_map/dot_general | solution.py:55
  106.8 9.9 %copy.24 = bf16[9,8,512,128]{3,2,1,0:T(8,128)(2,1)} copy(bf16[9,8,512,128]{3,1,2,0:T(8,128)(2,1)} %bitcast.63) | data formatting | bytes 18874368
  116.7 8.4 %slice.29 = bf16[70,512,128]{2,1,0:T(8,128)(2,1)} slice(bf16[72,512,128]{2,1,0:T(8,128)(2,1)} %bitcast.65), slice={[0:70], [0:512], [0:128]} | slice | bytes 18350080
  125.1 9.1 %gather_fusion.1 = bf16[64,2,2,128,128]{4,3,2,1,0:T(8,128)(2,1)} fusion(bf16[70,2,2,128,128]{4,3,2,1,0:T(8,128)(2,1)} %bitcast.66, s32[1024]{0:T(1024)S(1)} %pad_clamp_fusion), kind=kCustom, calls=%fused_computation.1 | custom fusion | bytes 16777472 | tf_op jit(solution)/shard_map/gather | solution.py:67
  134.2 3.8 %fusion.17 = (bf16[8,8,2,1,128,128]{5,4,3,2,1,0:T(8,128)(2,1)S(1)}, bf16[8,8,2,1,128,128]{5,4,3,2,1,0:T(8,128)(2,1)S(1)}) fusion(bf16[8,8,2,2,128,128]{5,4,3,2,1,0:T(8,128)(2,1)} %bitcast.68), kind=kLoop, calls=%fused_computation.49 | loop fusion | bytes 16777216 | tf_op jit(solution)/shard_map/slice | solution.py:68
  138.1 0.6 copy.19
  138.7 1.2 fusion.8
  139.8 0.3 fusion.18
  140.1 2.2 %copy.20 = bf16[8,8,2,1,128,128]{5,4,1,2,0,3:T(8,128)(2,1)} copy(bf16[8,8,2,1,128,128]{5,4,3,2,1,0:T(8,128)(2,1)S(1)} %get-tuple-element.3) | data formatting | bytes 8388608
  142.3 2.9 %fusion.9 = bf16[1,8,16,128]{3,2,1,0:T(8,128)(2,1)S(1)} fusion(bf16[8,2,1024,128]{3,2,1,0:T(8,128)(2,1)} %bitcast.69, f32[8,2,8]{2,1,0:T(2,128)S(1)} %fusion.18, f32[8,2,8,1024]{3,2,1,0:T(8,128)S(1)} %fusion.8), kind=kOutput, calls=%fused_computation.15 | convolution fusion | flops 33965184 | bytes 4751872 | tf_op jit(solution)/shard_map/skgt,sktd->skgd/dot_general | solution.py:85
  145.3 2.2 %collective-permute-start = (bf16[8,2048]{1,0:T(8,128)(2,1)S(1)}, bf16[8,2048]{1,0:T(8,128)(2,1)S(1)}, u32[]{:S(2)}, u32[]{:S(2)}) collective-permute-start(bf16[8,2048]{1,0:T(8,128)(2,1)S(1)} %bitcast.73), channel_id=1, source_target_pairs={{0,4},{4,8},{8,12},{12,16},{16,20},{20,24},{24,28},{28,0},{1,5},{5... | collective-permute-start | bytes 98312 | tf_op jit(solution)/shard_map/ppermute | solution.py:18
  147.5 3.3 %collective-permute-done = bf16[8,2048]{1,0:T(8,128)(2,1)S(1)} collective-permute-done((bf16[8,2048]{1,0:T(8,128)(2,1)S(1)}, bf16[8,2048]{1,0:T(8,128)(2,1)S(1)}, u32[]{:S(2)}, u32[]{:S(2)}) %collective-permute-start) | collective-permute-done | bytes 32800 | tf_op jit(solution)/shard_map/ppermute | solution.py:18
  150.8 0.0 collective-permute-start.1
  150.8 5.5 %collective-permute-done.1 = bf16[8,2048]{1,0:T(8,128)(2,1)S(1)} collective-permute-done((bf16[8,2048]{1,0:T(8,128)(2,1)S(1)}, bf16[8,2048]{1,0:T(8,128)(2,1)S(1)}, u32[]{:S(2)}, u32[]{:S(2)}) %collective-permute-start.1) | collective-permute-done | bytes 32800 | tf_op jit(solution)/shard_map/ppermute | solution.py:18
  156.3 0.0 collective-permute-start.2
  156.3 5.5 %collective-permute-done.2 = bf16[8,2048]{1,0:T(8,128)(2,1)S(1)} collective-permute-done((bf16[8,2048]{1,0:T(8,128)(2,1)S(1)}, bf16[8,2048]{1,0:T(8,128)(2,1)S(1)}, u32[]{:S(2)}, u32[]{:S(2)}) %collective-permute-start.2) | collective-permute-done | bytes 32800 | tf_op jit(solution)/shard_map/ppermute | solution.py:18
  161.7 0.0 collective-permute-start.3
  161.7 5.5 %collective-permute-done.3 = bf16[8,2048]{1,0:T(8,128)(2,1)S(1)} collective-permute-done((bf16[8,2048]{1,0:T(8,128)(2,1)S(1)}, bf16[8,2048]{1,0:T(8,128)(2,1)S(1)}, u32[]{:S(2)}, u32[]{:S(2)}) %collective-permute-start.3) | collective-permute-done | bytes 32800 | tf_op jit(solution)/shard_map/ppermute | solution.py:18
  167.2 0.0 collective-permute-start.4
  167.2 5.5 %collective-permute-done.4 = bf16[8,2048]{1,0:T(8,128)(2,1)S(1)} collective-permute-done((bf16[8,2048]{1,0:T(8,128)(2,1)S(1)}, bf16[8,2048]{1,0:T(8,128)(2,1)S(1)}, u32[]{:S(2)}, u32[]{:S(2)}) %collective-permute-start.4) | collective-permute-done | bytes 32800 | tf_op jit(solution)/shard_map/ppermute | solution.py:18
  172.6 0.0 collective-permute-start.5
  172.7 5.5 %collective-permute-done.5 = bf16[8,2048]{1,0:T(8,128)(2,1)S(1)} collective-permute-done((bf16[8,2048]{1,0:T(8,128)(2,1)S(1)}, bf16[8,2048]{1,0:T(8,128)(2,1)S(1)}, u32[]{:S(2)}, u32[]{:S(2)}) %collective-permute-start.5) | collective-permute-done | bytes 32800 | tf_op jit(solution)/shard_map/ppermute | solution.py:18
  178.1 0.0 collective-permute-start.6
  178.1 5.5 %collective-permute-done.6 = bf16[8,2048]{1,0:T(8,128)(2,1)S(1)} collective-permute-done((bf16[8,2048]{1,0:T(8,128)(2,1)S(1)}, bf16[8,2048]{1,0:T(8,128)(2,1)S(1)}, u32[]{:S(2)}, u32[]{:S(2)}) %collective-permute-start.6) | collective-permute-done | bytes 32800 | tf_op jit(solution)/shard_map/ppermute | solution.py:18
  183.6 3.0 %fusion.19 = f32[64,1024]{1,0:T(8,128)S(1)} fusion(bf16[64,2048]{1,0:T(8,128)(2,1)S(1)} %constant_dynamic-update-slice_fusion, bf16[2048,1024]{1,0:T(8,128)(2,1)} %param.13), kind=kOutput, calls=%fused_computation.51 | convolution fusion | flops 268435456 | bytes 4718592 | tf_op jit(solution)/shard_map/dot_general | solution.py:91
  186.6 23.9 %all-reduce.1 = bf16[64,1024]{1,0:T(8,128)(2,1)} all-reduce(f32[64,1024]{1,0:T(8,128)S(1)} %fusion.19), channel_id=1, replica_groups=mesh['dp'=8,'tensor'=4] {'tensor'}, use_global_device_ids=true, to_apply=%region_5.6 | all-reduce | flops 65536 | bytes 393216 | tf_op jit(solution)/shard_map/psum | solution.py:94
  (19 shorter events, 0.1 us)
Async XLA Ops:
  0.6 138.0 %copy-start = (bf16[8,16,128]{2,1,0:T(8,128)(2,1)S(1)}, bf16[8,16,128]{2,1,0:T(8,128)(2,1)}, u32[]{:S(2)}) copy-start(bf16[8,16,128]{2,1,0:T(8,128)(2,1)} %param.7) | copy-start | bytes 98308
  3.7 40.1 %all-to-all-start = ((bf16[8,2,1]{1,2,0:T(2,128)(2,1)}), bf16[8,2,1]{1,2,0:T(2,128)(2,1)S(1)}, u32[]{:S(2)}, u32[]{:S(2)}) async-start(bf16[8,2,1]{1,2,0:T(2,128)(2,1)} %convert_element_type.79), calls=%async_computation | async-start | bytes 8192 | tf_op jit(solution)/shard_map/all_to_all | solution.py:51
  41.8 7.3 %copy-start.1 = (s32[8,8]{1,0:T(8,128)S(1)}, s32[8,8]{1,0:T(8,128)}, u32[]{:S(2)}) copy-start(s32[8,8]{1,0:T(8,128)} %param.11) | copy-start | bytes 772
  41.8 7.4 %copy-start.2 = (s32[8]{0:T(128)S(1)}, s32[8]{0:T(128)}, u32[]{:S(2)}) copy-start(s32[8]{0:T(128)} %param.12) | copy-start | bytes 100
  43.7 52.3 %all-to-all-start.1 = ((bf16[16,2,2,128,128]{4,3,2,1,0:T(8,128)(2,1)}), bf16[16,2,2,128,128]{4,3,2,1,0:T(8,128)(2,1)S(1)}, u32[]{:S(2)}, u32[]{:S(2)}) async-start(bf16[16,2,2,128,128]{4,3,2,1,0:T(8,128)(2,1)} %bitcast.24), calls=%async_computation.1 | async-start | bytes 4194304 | tf_op jit(solution)/shard_map/all_to_all | solution.py:50
  145.3 5.5 %collective-permute-start = (bf16[8,2048]{1,0:T(8,128)(2,1)S(1)}, bf16[8,2048]{1,0:T(8,128)(2,1)S(1)}, u32[]{:S(2)}, u32[]{:S(2)}) collective-permute-start(bf16[8,2048]{1,0:T(8,128)(2,1)S(1)} %bitcast.73), channel_id=1, source_target_pairs={{0,4},{4,8},{8,12},{12,16},{16,20},{20,24},{24,28},{28,0},{1,5},{5... | collective-permute-start | bytes 98312 | tf_op jit(solution)/shard_map/ppermute | solution.py:18
  150.8 5.5 %collective-permute-start.1 = (bf16[8,2048]{1,0:T(8,128)(2,1)S(1)}, bf16[8,2048]{1,0:T(8,128)(2,1)S(1)}, u32[]{:S(2)}, u32[]{:S(2)}) collective-permute-start(bf16[8,2048]{1,0:T(8,128)(2,1)S(1)} %collective-permute-done), channel_id=1, source_target_pairs={{0,4},{4,8},{8,12},{12,16},{16,20},{20,24},{24,28},{28,0},{1,5},{5... | collective-permute-start | bytes 98312 | tf_op jit(solution)/shard_map/ppermute | solution.py:18
  156.3 5.5 %collective-permute-start.2 = (bf16[8,2048]{1,0:T(8,128)(2,1)S(1)}, bf16[8,2048]{1,0:T(8,128)(2,1)S(1)}, u32[]{:S(2)}, u32[]{:S(2)}) collective-permute-start(bf16[8,2048]{1,0:T(8,128)(2,1)S(1)} %collective-permute-done.1), channel_id=1, source_target_pairs={{0,4},{4,8},{8,12},{12,16},{16,20},{20,24},{24,28},{28,0},{1,5},{5... | collective-permute-start | bytes 98312 | tf_op jit(solution)/shard_map/ppermute | solution.py:18
  161.7 5.5 %collective-permute-start.3 = (bf16[8,2048]{1,0:T(8,128)(2,1)S(1)}, bf16[8,2048]{1,0:T(8,128)(2,1)S(1)}, u32[]{:S(2)}, u32[]{:S(2)}) collective-permute-start(bf16[8,2048]{1,0:T(8,128)(2,1)S(1)} %collective-permute-done.2), channel_id=1, source_target_pairs={{0,4},{4,8},{8,12},{12,16},{16,20},{20,24},{24,28},{28,0},{1,5},{5... | collective-permute-start | bytes 98312 | tf_op jit(solution)/shard_map/ppermute | solution.py:18
  167.2 5.5 %collective-permute-start.4 = (bf16[8,2048]{1,0:T(8,128)(2,1)S(1)}, bf16[8,2048]{1,0:T(8,128)(2,1)S(1)}, u32[]{:S(2)}, u32[]{:S(2)}) collective-permute-start(bf16[8,2048]{1,0:T(8,128)(2,1)S(1)} %collective-permute-done.3), channel_id=1, source_target_pairs={{0,4},{4,8},{8,12},{12,16},{16,20},{20,24},{24,28},{28,0},{1,5},{5... | collective-permute-start | bytes 98312 | tf_op jit(solution)/shard_map/ppermute | solution.py:18
  172.6 5.5 %collective-permute-start.5 = (bf16[8,2048]{1,0:T(8,128)(2,1)S(1)}, bf16[8,2048]{1,0:T(8,128)(2,1)S(1)}, u32[]{:S(2)}, u32[]{:S(2)}) collective-permute-start(bf16[8,2048]{1,0:T(8,128)(2,1)S(1)} %collective-permute-done.4), channel_id=1, source_target_pairs={{0,4},{4,8},{8,12},{12,16},{16,20},{20,24},{24,28},{28,0},{1,5},{5... | collective-permute-start | bytes 98312 | tf_op jit(solution)/shard_map/ppermute | solution.py:18
  178.1 5.5 %collective-permute-start.6 = (bf16[8,2048]{1,0:T(8,128)(2,1)S(1)}, bf16[8,2048]{1,0:T(8,128)(2,1)S(1)}, u32[]{:S(2)}, u32[]{:S(2)}) collective-permute-start(bf16[8,2048]{1,0:T(8,128)(2,1)S(1)} %collective-permute-done.5), channel_id=1, source_target_pairs={{0,4},{4,8},{8,12},{12,16},{16,20},{20,24},{24,28},{28,0},{1,5},{5... | collective-permute-start | bytes 98312 | tf_op jit(solution)/shard_map/ppermute | solution.py:18
